TPU v7x, 32 devices: a whole 2x2x4 slice. The times are simulated.
32 devices in a mesh: band: 16 (over z, y, x), dp: 2 (over core).
Axes of the slice: x: 2, y: 2, z: 4, core: 2. Of those that a mesh axis runs over, the one named last changes fastest.
Arguments:
- pages: bfloat16 [32768, 256], P('band', 'dp'), may hold values from -6 to 6
- band_tiles: bfloat16 [256, 3, 128, 128], P('band'), may hold values from 0 to 1, as said below
- off_tiles: bfloat16 [256, 128, 128], P('band'), may hold values from 0 to 1, as said below
- off_row: int32 [256], P('band'), may hold values from 0 to 15
- requests: int32 [256], P('band'), may hold values from 0 to 15
- label_page: int32 [16384], P('band'), may hold values from 0 to 2047
- labels: int32 [16384], P(('band', 'dp')), may hold values from 0 to 255
- w_first: bfloat16 [768, 1024], replicated, may hold values from -0.21875 to 0.21875
- w_second: bfloat16 [1024, 256], replicated
Outputs:
- prop_a: bfloat16 [32768, 256], P('band', 'dp')
- prop_t: bfloat16 [32768, 256], P('band', 'dp')
- prop_aat: bfloat16 [32768, 256], P('band', 'dp')
- grad_w1: bfloat16 [768, 1024], replicated
- grad_w2: bfloat16 [1024, 256], replicated
Inputs may be any that keep to these rules, and one draw needn't show every extreme that they name: `off_row`: row block within a band. `requests`: row block within a band. `band_tiles`: links weighted between 0 and 1, about half of the entries zero. `off_tiles`: links weighted between 0 and 1, about half of the entries zero.
All inputs are finite; a program needn't handle non-finite values.
Results may differ from a plain program's by a relative error of at most 0.011.
Values may be sent and summed in bfloat16 or wider, within the bound.
A program may use at most 128 MiB of HBM per device.

v0:
```python
import jax
import jax.numpy as jnp
from jax import lax
from jax.sharding import PartitionSpec as P


def padded_2(cells, sides, width):
    for axis, dim in sides:
        count = lax.axis_size(axis)
        ends = count - 1
        head = lax.slice_in_dim(cells, 0, width, axis=dim)
        tail = lax.slice_in_dim(cells, cells.shape[dim] - width, cells.shape[dim], axis=dim)
        cells = jnp.concatenate(
            [
                lax.ppermute(tail, axis, [(i, (i + 1) % count) for i in range(ends)]),
                cells,
                lax.ppermute(head, axis, [((i + 1) % count, i) for i in range(ends)]),
            ],
            axis=dim,
        )
    return cells


def per_device(
    pages, band_tiles, off_tiles, off_row, requests, label_page, labels, w_first, w_second
):
    tile_size = band_tiles.shape[-1]
    rows_dev, feat_half = pages.shape
    block_count = rows_dev // tile_size
    block_iota = jnp.arange(block_count, dtype=jnp.int32)
    served = lax.all_to_all(requests, "band", split_axis=0, concat_axis=0, tiled=True)
    row_hot = (off_row[None, :] == block_iota[:, None]).astype(jnp.float32)
    served_hot = (served[None, :] == block_iota[:, None]).astype(jnp.float32)

    def band_forward(field):
        padded = padded_2(field, (("band", 0),), tile_size)
        blocks = padded.reshape(block_count + 2, tile_size, feat_half)
        windows = jnp.stack(
            [blocks[0:block_count], blocks[1 : block_count + 1], blocks[2 : block_count + 2]], 1
        )
        return jnp.einsum("rjab,rjbf->raf", band_tiles, windows, preferred_element_type=jnp.float32)

    def off_apply(fetched):
        products = jnp.einsum(
            "kab,kbf->kaf", off_tiles, fetched, preferred_element_type=jnp.float32
        )
        return jnp.einsum("rk,kaf->raf", row_hot, products, precision=lax.Precision.HIGHEST)

    def serve_blocks(field):
        return jnp.take(field.reshape(block_count, tile_size, feat_half), served, axis=0)

    own_blocks = pages.reshape(block_count, tile_size, feat_half)
    near_part = band_forward(pages)
    adjoint_terms = jnp.einsum(
        "rjab,raf->rjbf", band_tiles, own_blocks, preferred_element_type=jnp.float32
    )
    accumulated = jnp.zeros((block_count + 2, tile_size, feat_half), jnp.float32)
    accumulated = accumulated.at[0:block_count].add(adjoint_terms[:, 0])
    accumulated = accumulated.at[1 : block_count + 1].add(adjoint_terms[:, 1])
    accumulated = accumulated.at[2 : block_count + 2].add(adjoint_terms[:, 2])
    rim_rows = jnp.concatenate([accumulated[0], accumulated[block_count + 1]], 0)
    received = padded_2(rim_rows, (("band", 0),), tile_size)
    inner_part = accumulated[1 : block_count + 1]
    inner_part = inner_part.at[0].add(received[0:tile_size])
    inner_part = inner_part.at[block_count - 1].add(received[3 * tile_size : 4 * tile_size])
    back_terms = jnp.einsum(
        "kab,kaf->kbf",
        off_tiles,
        jnp.take(own_blocks, off_row, axis=0),
        preferred_element_type=jnp.float32,
    ).astype(jnp.bfloat16)
    outgoing = serve_blocks(pages)
    fetched = lax.all_to_all(outgoing, "band", split_axis=0, concat_axis=0, tiled=True)
    returned = lax.all_to_all(back_terms, "band", split_axis=0, concat_axis=0, tiled=True)
    prop_a = (near_part + off_apply(fetched)).reshape(rows_dev, feat_half).astype(jnp.bfloat16)
    back_sum = jnp.einsum(
        "rk,kbf->rbf", served_hot, returned.astype(jnp.float32), precision=lax.Precision.HIGHEST
    )
    prop_t = (inner_part + back_sum).reshape(rows_dev, feat_half).astype(jnp.bfloat16)
    fetched_again = lax.all_to_all(
        serve_blocks(prop_t), "band", split_axis=0, concat_axis=0, tiled=True
    )
    prop_aat = (
        (band_forward(prop_t) + off_apply(fetched_again))
        .reshape(rows_dev, feat_half)
        .astype(jnp.bfloat16)
    )
    picked = jnp.stack(
        [
            jnp.take(prop_a, label_page, axis=0),
            jnp.take(prop_t, label_page, axis=0),
            jnp.take(prop_aat, label_page, axis=0),
        ],
        0,
    )
    regrouped = lax.all_to_all(picked, "dp", split_axis=1, concat_axis=2, tiled=True)
    hidden_units = w_first.shape[1]
    w_first_split = w_first.reshape(3, regrouped.shape[2], hidden_units)
    pre_act = jnp.einsum(
        "krf,kfh->rh", regrouped, w_first_split, preferred_element_type=jnp.float32
    )
    sigma = jax.nn.sigmoid(pre_act)
    hidden = (pre_act * sigma).astype(jnp.bfloat16)
    logits = jnp.dot(hidden, w_second, preferred_element_type=jnp.float32)
    probabilities = jax.nn.softmax(logits, axis=-1)
    label_hot = (labels[:, None] == jnp.arange(w_second.shape[1], dtype=jnp.int32)[None, :]).astype(
        jnp.float32
    )
    errors = ((probabilities - label_hot) / label_page.shape[0]).astype(jnp.bfloat16)
    grad_second = jnp.dot(hidden.T, errors, preferred_element_type=jnp.float32)
    slope = sigma * (1.0 + pre_act * (1.0 - sigma))
    back_signal = (jnp.dot(errors, w_second.T, preferred_element_type=jnp.float32) * slope).astype(
        jnp.bfloat16
    )
    grad_first = jnp.einsum(
        "krf,rh->kfh", regrouped, back_signal, preferred_element_type=jnp.float32
    ).reshape(w_first.shape[0], hidden_units)
    summed_first, summed_second = lax.psum((grad_first, grad_second), ("band", "dp"))
    return (
        prop_a,
        prop_t,
        prop_aat,
        summed_first.astype(jnp.bfloat16),
        summed_second.astype(jnp.bfloat16),
    )


def solution(mesh):
    placed = (
        P("band", "dp"),
        P("band", None, None, None),
        P("band", None, None),
        P("band"),
        P("band"),
        P("band"),
        P(("band", "dp")),
        P(),
        P(),
    )
    return jax.shard_map(
        per_device,
        mesh=mesh,
        in_specs=placed,
        out_specs=(P("band", "dp"), P("band", "dp"), P("band", "dp"), P(), P()),
        check_vma=False,
    )
```

profile of v0, /device:TPU:0, one launch (start us, length us, event | category | flops | bytes accessed | tf_op | source)
XLA Modules:
  0.0 221.8 jit_solution(7156766890405385631)
XLA Ops:
  2.1 8.3 %all-to-all-start = ((s32[16,1,1]{2,1,0:T(1,128)}), s32[16,1,1]{2,1,0:T(1,128)S(1)}, u32[]{:S(2)}, u32[]{:S(2)}) async-start(s32[16,1,1]{2,1,0:T(1,128)} %copy.47), calls=%async_computation | async-start | bytes 16384 | tf_op jit(solution)/shard_map/all_to_all | solution.py:31
  11.2 3.8 %collective-permute-start = (bf16[128,128]{1,0:T(8,128)(2,1)S(1)}, bf16[128,128]{1,0:T(8,128)(2,1)S(1)}, u32[]{:S(2)}, u32[]{:S(2)}) collective-permute-start(bf16[128,128]{1,0:T(8,128)(2,1)S(1)} %get-tuple-element.77), channel_id=1, source_target_pairs={{0,2},{2,4},{4,6},{6,8},{8,10},{10,12},{12,14},{14,16},{16,18},{18... | collective-permute-start | bytes 98312 | tf_op jit(solution)/shard_map/ppermute | solution.py:15
  16.3 2.1 fusion.78
  19.1 4.5 %collective-permute-start.2 = (f32[128,128]{1,0:T(8,128)S(1)}, f32[128,128]{1,0:T(8,128)S(1)}, u32[]{:S(2)}, u32[]{:S(2)}) collective-permute-start(f32[128,128]{1,0:T(8,128)S(1)} %slice_bitcast_fusion.4), channel_id=1, source_target_pairs={{0,2},{2,4},{4,6},{6,8},{8,10},{10,12},{12,14},{14,16},{16,18},{18... | collective-permute-start | bytes 196616 | tf_op jit(solution)/shard_map/ppermute | solution.py:15
  26.3 2.4 %fusion.46 = bf16[16,128,128]{1,2,0:T(8,128)(2,1)} fusion(bf16[16,128,128]{2,1,0:T(8,128)(2,1)} %param.25, bf16[16,128,128]{2,1,0:T(8,128)(2,1)} %gather_fusion.1, pred[16]{0:T(512)(128)(4,1)} %compare_and_fusion.1), kind=kOutput, calls=%fused_computation.40 | convolution fusion | flops 67633152 | bytes 1572880 | tf_op jit(solution)/shard_map/kab,kaf->kbf/dot_general | solution.py:66
  28.8 2.0 copy.55
  31.9 7.4 %all-to-all-start.2 = ((bf16[16,128,128]{2,1,0:T(8,128)(2,1)}), bf16[16,128,128]{2,1,0:T(8,128)(2,1)}, u32[]{:S(2)}, u32[]{:S(2)}) async-start(bf16[16,128,128]{2,1,0:T(8,128)(2,1)} %copy.55), calls=%async_computation.2 | async-start | bytes 1048576 | tf_op jit(solution)/shard_map/all_to_all | solution.py:74
  42.9 2.0 copy.48
  49.9 3.8 %collective-permute-done.3 = f32[128,128]{1,0:T(8,128)S(1)} collective-permute-done((f32[128,128]{1,0:T(8,128)S(1)}, f32[128,128]{1,0:T(8,128)S(1)}, u32[]{:S(2)}, u32[]{:S(2)}) %collective-permute-start.3) | collective-permute-done | bytes 65568 | tf_op jit(solution)/shard_map/ppermute | solution.py:17
  55.1 7.8 %all-to-all-start.1 = ((bf16[16,128,128]{1,2,0:T(8,128)(2,1)}), bf16[16,128,128]{1,2,0:T(8,128)(2,1)}, u32[]{:S(2)}, u32[]{:S(2)}) async-start(bf16[16,128,128]{1,2,0:T(8,128)(2,1)} %broadcast_select_fusion.1), calls=%async_computation.1 | async-start | bytes 1048576 | tf_op jit(solution)/shard_map/all_to_all | solution.py:73
  66.3 3.8 %collective-permute-start.4 = (bf16[128,128]{1,0:T(8,128)(2,1)S(1)}, bf16[128,128]{1,0:T(8,128)(2,1)S(1)}, u32[]{:S(2)}, u32[]{:S(2)}) collective-permute-start(bf16[128,128]{1,0:T(8,128)(2,1)S(1)} %get-tuple-element.73), channel_id=1, source_target_pairs={{0,2},{2,4},{4,6},{6,8},{8,10},{10,12},{12,14},{14,16},{16,18},{18... | collective-permute-start | bytes 98312 | tf_op jit(solution)/shard_map/ppermute | solution.py:15
  71.4 3.2 %gather_fusion.4 = bf16[1024,128]{1,0:T(8,128)(2,1)S(1)} fusion(bf16[2048,128]{1,0:T(8,128)(2,1)S(1)} %bitcast.130, s32[1024]{0:T(1024)S(1)} %fusion.70), kind=kCustom, calls=%fused_computation.4.clone | custom fusion | bytes 528384 | tf_op jit(solution)/shard_map/jit(_take)/gather | solution.py:91
  76.6 7.7 %all-to-all-start.3 = ((bf16[16,128,128]{2,1,0:T(8,128)(2,1)}), bf16[16,128,128]{2,1,0:T(8,128)(2,1)}, u32[]{:S(2)}, u32[]{:S(2)}) async-start(bf16[16,128,128]{2,1,0:T(8,128)(2,1)} %broadcast_select_fusion), calls=%async_computation.3 | async-start | bytes 1048576 | tf_op jit(solution)/shard_map/all_to_all | solution.py:80
  84.3 2.5 %convolution_bitcast_fusion.1 = f32[16,128,128]{1,2,0:T(8,128)} fusion(bf16[16,128,128]{1,2,0:T(8,128)(2,1)} %all-to-all-done.1, bf16[16,128,128]{2,1,0:T(8,128)(2,1)S(1)} %copy-done.5), kind=kOutput, calls=%fused_computation.33 | convolution fusion | flops 67108864 | bytes 2097152 | tf_op jit(solution)/shard_map/kab,kbf->kaf/dot_general | solution.py:44
  86.8 2.6 %copy.49 = f32[16,128,128]{2,0,1:T(8,128)} copy(f32[16,128,128]{1,2,0:T(8,128)} %convolution_bitcast_fusion.1) | data formatting | bytes 2097152 | tf_op jit(solution)/shard_map/kab,kbf->kaf/dot_general | solution.py:44
  89.4 2.0 fusion.63
  93.3 4.3 %gather_fusion.3 = bf16[1024,128]{1,0:T(8,128)(2,1)} fusion(bf16[2048,128]{1,0:T(8,128)(2,1)S(1)} %bitcast.138, s32[1024]{0:T(1024)S(1)} %fusion.70), kind=kCustom, calls=%fused_computation.1.clone | custom fusion | bytes 528384 | tf_op jit(solution)/shard_map/jit(_take)/gather | solution.py:90
  98.6 2.5 %convolution_bitcast_fusion = f32[16,128,128]{1,2,0:T(8,128)} fusion(bf16[16,128,128]{2,1,0:T(8,128)(2,1)} %all-to-all-done.3, bf16[16,128,128]{2,1,0:T(8,128)(2,1)S(1)} %copy-done.6), kind=kOutput, calls=%fused_computation.32 | convolution fusion | flops 67108864 | bytes 2097152 | tf_op jit(solution)/shard_map/kab,kbf->kaf/dot_general | solution.py:44
  101.1 2.6 %copy.60 = f32[16,128,128]{2,0,1:T(8,128)} copy(f32[16,128,128]{1,2,0:T(8,128)} %convolution_bitcast_fusion) | data formatting | bytes 2097152 | tf_op jit(solution)/shard_map/kab,kbf->kaf/dot_general | solution.py:44
  107.7 3.2 %gather_fusion.5 = bf16[1024,128]{1,0:T(8,128)(2,1)S(1)} fusion(bf16[2048,128]{1,0:T(8,128)(2,1)S(1)} %bitcast.140, s32[1024]{0:T(1024)S(1)} %fusion.70), kind=kCustom, calls=%fused_computation.5.clone | custom fusion | bytes 528384 | tf_op jit(solution)/shard_map/jit(_take)/gather | solution.py:92
  111.9 4.6 %all_to_all.45 = bf16[3,1024,128]{2,0,1:T(4,128)(2,1)S(1)} all-to-all(bf16[3,1024,128]{2,0,1:T(4,128)(2,1)S(1)} %copy.62), channel_id=1, replica_groups=mesh['band'=16,'dp'=2] {'dp'}, dimensions={1} | all-to-all | bytes 1572864 | tf_op jit(solution)/shard_map/all_to_all | solution.py:96
  119.1 2.5 %fusion.3 = (bf16[512,1024]{1,0:T(8,128)(2,1)S(1)}, f32[512,1024,1]{1,0,2:T(8,128)}) fusion(bf16[3,512,256]{2,1,0:T(8,128)(2,1)S(1)} %all_to_all.39, bf16[3,256,1024]{2,1,0:T(8,128)(2,1)S(1)} %bitcast.129), kind=kOutput, calls=%fused_computation.12 | convolution fusion | flops 807927808 | bytes 5505024 | tf_op jit(solution)/shard_map/krf,kfh->rh/dot_general | solution.py:99
  122.9 5.4 %fusion.21 = f32[768,1024]{1,0:T(8,128)} fusion(bf16[768,512]{1,0:T(8,128)(2,1)} %bitcast.145, f32[512,1024,1]{1,0,2:T(8,128)} %get-tuple-element.83, bf16[1024,256]{1,0:T(8,128)(2,1)} %param.31, f32[512,256]{0,1:T(8,128)S(1)} %get-tuple-element.85, s32[512]{0:T(512)S(1)} %copy-done.19, f32[512]{0:T(512)S(1)} %fusion.56, f32[512]{0:T(512)S(1)} %get-tuple-element.84), kind=kOutput, calls=%fused_computation.30 | convolution fusion | flops 1079377920 | bytes 7084032 | tf_op jit(solution)/shard_map/krf,rh->kfh/dot_general | solution.py:115
  128.3 93.5 %all-reduce.3 = (bf16[768,1024]{1,0:T(8,128)(2,1)}, bf16[1024,256]{1,0:T(8,128)(2,1)}) all-reduce(f32[768,1024]{1,0:T(8,128)} %fusion.21, f32[1024,256]{1,0:T(8,128)S(1)} %fusion.75), channel_id=1, replica_groups=mesh['band'=16,'dp'=2] {'band','dp'}, use_global_device_ids=true, to_apply=%region_2.5 | all-reduce | flops 1048576 | bytes 6291456 | tf_op jit(solution)/shard_map/psum | solution.py:118
  (94 shorter events, 36.0 us)
Async XLA Ops:
  0.6 118.5 %copy-start = (bf16[768,1024]{1,0:T(8,128)(2,1)S(1)}, bf16[768,1024]{1,0:T(8,128)(2,1)}, u32[]{:S(2)}) copy-start(bf16[768,1024]{1,0:T(8,128)(2,1)} %param.30) | copy-start | bytes 4718596
  2.1 29.8 %all-to-all-start = ((s32[16,1,1]{2,1,0:T(1,128)}), s32[16,1,1]{2,1,0:T(1,128)S(1)}, u32[]{:S(2)}, u32[]{:S(2)}) async-start(s32[16,1,1]{2,1,0:T(1,128)} %copy.47), calls=%async_computation | async-start | bytes 16384 | tf_op jit(solution)/shard_map/all_to_all | solution.py:31
  11.2 37.6 %collective-permute-start = (bf16[128,128]{1,0:T(8,128)(2,1)S(1)}, bf16[128,128]{1,0:T(8,128)(2,1)S(1)}, u32[]{:S(2)}, u32[]{:S(2)}) collective-permute-start(bf16[128,128]{1,0:T(8,128)(2,1)S(1)} %get-tuple-element.77), channel_id=1, source_target_pairs={{0,2},{2,4},{4,6},{6,8},{8,10},{10,12},{12,14},{14,16},{16,18},{18... | collective-permute-start | bytes 98312 | tf_op jit(solution)/shard_map/ppermute | solution.py:15
  15.0 33.8 %collective-permute-start.1 = (bf16[128,128]{1,0:T(8,128)(2,1)S(1)}, bf16[128,128]{1,0:T(8,128)(2,1)S(1)}, u32[]{:S(2)}, u32[]{:S(2)}) collective-permute-start(bf16[128,128]{1,0:T(8,128)(2,1)S(1)} %get-tuple-element.78), channel_id=1, source_target_pairs={{2,0},{4,2},{6,4},{8,6},{10,8},{12,10},{14,12},{16,14},{18,16},{20... | collective-permute-start | bytes 98312 | tf_op jit(solution)/shard_map/ppermute | solution.py:17
  18.9 4.8 %copy-start.16 = (s32[16]{0:T(128)S(1)}, s32[16]{0:T(128)}, u32[]{:S(2)}) copy-start(s32[16]{0:T(128)} %param.26) | copy-start | bytes 196
  19.0 5.3 %copy-start.14 = (s32[1024]{0:T(1024)S(1)}, s32[1024]{0:T(1024)}, u32[]{:S(2)}) copy-start(s32[1024]{0:T(1024)} %param.28) | copy-start | bytes 12292
  19.0 6.0 %copy-start.2 = (bf16[2048,128]{1,0:T(8,128)(2,1)S(1)}, bf16[2048,128]{1,0:T(8,128)(2,1)}, u32[]{:S(2)}) copy-start(bf16[2048,128]{1,0:T(8,128)(2,1)} %param.23) | copy-start | bytes 1572868
  19.1 27.7 %collective-permute-start.2 = (f32[128,128]{1,0:T(8,128)S(1)}, f32[128,128]{1,0:T(8,128)S(1)}, u32[]{:S(2)}, u32[]{:S(2)}) collective-permute-start(f32[128,128]{1,0:T(8,128)S(1)} %slice_bitcast_fusion.4), channel_id=1, source_target_pairs={{0,2},{2,4},{4,6},{6,8},{8,10},{10,12},{12,14},{14,16},{16,18},{18... | collective-permute-start | bytes 196616 | tf_op jit(solution)/shard_map/ppermute | solution.py:15
  31.9 23.3 %all-to-all-start.2 = ((bf16[16,128,128]{2,1,0:T(8,128)(2,1)}), bf16[16,128,128]{2,1,0:T(8,128)(2,1)}, u32[]{:S(2)}, u32[]{:S(2)}) async-start(bf16[16,128,128]{2,1,0:T(8,128)(2,1)} %copy.55), calls=%async_computation.2 | async-start | bytes 1048576 | tf_op jit(solution)/shard_map/all_to_all | solution.py:74
  44.9 18.0 %copy-start.18 = (s32[16]{0:T(128)S(1)}, s32[16]{0:T(128)}, u32[]{:S(2)}) copy-start(s32[16]{0:T(128)} %reduce.10) | copy-start | bytes 196
  47.5 6.1 %collective-permute-start.3 = (f32[128,128]{1,0:T(8,128)S(1)}, f32[128,128]{1,0:T(8,128)S(1)}, u32[]{:S(2)}, u32[]{:S(2)}) collective-permute-start(f32[128,128]{1,0:T(8,128)S(1)} %get-tuple-element.69), channel_id=1, source_target_pairs={{2,0},{4,2},{6,4},{8,6},{10,8},{12,10},{14,12},{16,14},{18,16},{20... | collective-permute-start | bytes 196616 | tf_op jit(solution)/shard_map/ppermute | solution.py:17
  55.1 21.4 %all-to-all-start.1 = ((bf16[16,128,128]{1,2,0:T(8,128)(2,1)}), bf16[16,128,128]{1,2,0:T(8,128)(2,1)}, u32[]{:S(2)}, u32[]{:S(2)}) async-start(bf16[16,128,128]{1,2,0:T(8,128)(2,1)} %broadcast_select_fusion.1), calls=%async_computation.1 | async-start | bytes 1048576 | tf_op jit(solution)/shard_map/all_to_all | solution.py:73
  64.9 40.9 %copy-start.1 = (bf16[16,128,128]{2,1,0:T(8,128)(2,1)}, bf16[16,128,128]{2,1,0:T(8,128)(2,1)S(1)}, u32[]{:S(2)}) copy-start(bf16[16,128,128]{2,1,0:T(8,128)(2,1)S(1)} %fusion.50) | copy-start | bytes 1572868
  66.3 31.3 %collective-permute-start.4 = (bf16[128,128]{1,0:T(8,128)(2,1)S(1)}, bf16[128,128]{1,0:T(8,128)(2,1)S(1)}, u32[]{:S(2)}, u32[]{:S(2)}) collective-permute-start(bf16[128,128]{1,0:T(8,128)(2,1)S(1)} %get-tuple-element.73), channel_id=1, source_target_pairs={{0,2},{2,4},{4,6},{6,8},{8,10},{10,12},{12,14},{14,16},{16,18},{18... | collective-permute-start | bytes 98312 | tf_op jit(solution)/shard_map/ppermute | solution.py:15
  70.1 27.5 %collective-permute-start.5 = (bf16[128,128]{1,0:T(8,128)(2,1)S(1)}, bf16[128,128]{1,0:T(8,128)(2,1)S(1)}, u32[]{:S(2)}, u32[]{:S(2)}) collective-permute-start(bf16[128,128]{1,0:T(8,128)(2,1)S(1)} %get-tuple-element.74), channel_id=1, source_target_pairs={{2,0},{4,2},{6,4},{8,6},{10,8},{12,10},{14,12},{16,14},{18,16},{20... | collective-permute-start | bytes 98312 | tf_op jit(solution)/shard_map/ppermute | solution.py:17
  71.4 12.9 %copy-start.5 = (bf16[16,128,128]{2,1,0:T(8,128)(2,1)S(1)}, bf16[16,128,128]{2,1,0:T(8,128)(2,1)}, u32[]{:S(2)}) copy-start(bf16[16,128,128]{2,1,0:T(8,128)(2,1)} %param.25) | copy-start | bytes 1572868
  76.6 22.0 %all-to-all-start.3 = ((bf16[16,128,128]{2,1,0:T(8,128)(2,1)}), bf16[16,128,128]{2,1,0:T(8,128)(2,1)}, u32[]{:S(2)}, u32[]{:S(2)}) async-start(bf16[16,128,128]{2,1,0:T(8,128)(2,1)} %broadcast_select_fusion), calls=%async_computation.3 | async-start | bytes 1048576 | tf_op jit(solution)/shard_map/all_to_all | solution.py:80
  84.3 5.1 %copy-start.17 = (s32[16]{0:T(128)S(1)}, s32[16]{0:T(128)}, u32[]{:S(2)}) copy-start(s32[16]{0:T(128)} %param.26) | copy-start | bytes 196
  93.3 7.9 %copy-start.3 = (bf16[16,128,128]{2,1,0:T(8,128)(2,1)}, bf16[16,128,128]{2,1,0:T(8,128)(2,1)S(1)}, u32[]{:S(2)}) copy-start(bf16[16,128,128]{2,1,0:T(8,128)(2,1)S(1)} %fusion.43) | copy-start | bytes 1572868
  93.3 5.3 %copy-start.6 = (bf16[16,128,128]{2,1,0:T(8,128)(2,1)S(1)}, bf16[16,128,128]{2,1,0:T(8,128)(2,1)}, u32[]{:S(2)}) copy-start(bf16[16,128,128]{2,1,0:T(8,128)(2,1)} %param.25) | copy-start | bytes 1572868
  107.6 3.6 %copy-start.4 = (bf16[16,128,128]{2,1,0:T(8,128)(2,1)}, bf16[16,128,128]{2,1,0:T(8,128)(2,1)S(1)}, u32[]{:S(2)}) copy-start(bf16[16,128,128]{2,1,0:T(8,128)(2,1)S(1)} %fusion.38) | copy-start | bytes 1572868
  107.6 3.2 %copy-start.10 = (bf16[1024,128]{1,0:T(8,128)(2,1)S(1)}, bf16[1024,128]{1,0:T(8,128)(2,1)}, u32[]{:S(2)}) copy-start(bf16[1024,128]{1,0:T(8,128)(2,1)} %gather_fusion.3) | copy-start | bytes 786436
  107.7 3.2 %copy-start.15 = (pred[1024]{0:T(1024)(128)(4,1)S(1)}, pred[1024]{0:T(1024)(128)(4,1)}, u32[]{:S(2)}) copy-start(pred[1024]{0:T(1024)(128)(4,1)} %compare_and_fusion) | copy-start | bytes 3076
  119.1 2.5 %copy-start.11 = (bf16[1024,256]{1,0:T(8,128)(2,1)S(1)}, bf16[1024,256]{1,0:T(8,128)(2,1)}, u32[]{:S(2)}) copy-start(bf16[1024,256]{1,0:T(8,128)(2,1)} %param.31) | copy-start | bytes 1572868
  (6 other events, 10.2 us)
where the time goes:
time: 223 us; the launch traced here: 222 us
  blocking collectives  98 us (44%)
  starting transfers between devices  47.2 us (21%)
  local copies, waits for them, and re-layouts  31.2 us (14%)
  matrix products  27.8 us (12%)
  other arithmetic  12.6 us (6%)
  waiting for transfers between devices  3.83 us (2%)
    psum x1, blocking collectives, per_device(): lax.psum((grad_first, grad_second), ('band', 'dp'))  93.5 us
    ppermute x3, starting transfers between devices, padded_2(): lax.ppermute(tail, axis, [(i, (i + 1) % count) for i in range(ends)])  12.1 us
    all_to_all x1, starting transfers between devices, per_device(): lax.all_to_all(requests, 'band', split_axis=0, concat_axis=0, tiled=True)  8.31 us
    all_to_all x1, starting transfers between devices, per_device(): lax.all_to_all(outgoing, 'band', split_axis=0, concat_axis=0, tiled=True)  7.81 us
    all_to_all x1, starting transfers between devices, per_device(): lax.all_to_all(serve_blocks(prop_t), 'band', split_axis=0, concat_axis=0,...  7.68 us
    all_to_all x1, starting transfers between devices, per_device(): lax.all_to_all(back_terms, 'band', split_axis=0, concat_axis=0, tiled=True)  7.4 us
    dot_general x1, matrix products, per_device(): jnp.einsum('krf,rh->kfh', regrouped, back_signal, preferred_element_type=...  5.42 us
    dot_general x2, local copies, waits for them, and re-layouts, off_apply(): jnp.einsum('kab,kbf->kaf', off_tiles, fetched, preferred_element_type=jnp...  5.22 us
  transfers between devices with their start and end apart: 10, of which 1 were waited for; matrix products, arithmetic and copies ran while one was open for 20% of the time, Pallas kernels for 0%

commit v1 on v0

--- a/solution.py
+++ b/solution.py
@@ -115,7 +115,8 @@
     grad_first = jnp.einsum(
         "krf,rh->kfh", regrouped, back_signal, preferred_element_type=jnp.float32
     ).reshape(w_first.shape[0], hidden_units)
-    summed_first, summed_second = lax.psum((grad_first, grad_second), ("band", "dp"))
+    view_leaves_up = lambda work_x: lax.psum(lax.psum(work_x, axis_name="dp"), "band")
+    summed_first, summed_second = view_leaves_up((grad_first, grad_second))
     return (
         prop_a,
         prop_t,

time: 223 us -> 354 us (1.59)
  blocking collectives: 98 us -> 185 us
  waiting for transfers between devices: 3.83 us -> 33.8 us
  between operations: 1.12 us -> 14.5 us
    psum x1, blocking collectives: 93.5 us -> 181 us  [per_device(): lax.psum(lax.psum(work_x, axis_name='dp'), 'band')]
    psum x0 -> x1, waiting for transfers between devices: none -> 30 us  [per_device(): lax.psum(work_x, axis_name='dp')]
  transfers between devices with their start and end apart: 10 -> 11, of which waited for: 1 -> 2; matrix products, arithmetic and copies ran while one was open for 20% -> 13% of each run, Pallas kernels for 0% -> 0%
where the time goes in v1:
time: 354 us; the launch traced here: 353 us
  blocking collectives  185 us (52%)
  starting transfers between devices  47.2 us (13%)
  waiting for transfers between devices  33.8 us (10%)
  local copies, waits for them, and re-layouts  31.2 us (9%)
  matrix products  28.3 us (8%)
  between operations  14.5 us (4%)
  other arithmetic  12.4 us (4%)
    psum x1, blocking collectives, per_device(): lax.psum(lax.psum(work_x, axis_name='dp'), 'band')  181 us
    psum x1, waiting for transfers between devices, per_device(): lax.psum(work_x, axis_name='dp')  30 us
    ppermute x3, starting transfers between devices, padded_2(): lax.ppermute(tail, axis, [(i, (i + 1) % count) for i in range(ends)])  12.1 us
    all_to_all x1, starting transfers between devices, per_device(): lax.all_to_all(requests, 'band', split_axis=0, concat_axis=0, tiled=True)  8.31 us
    all_to_all x1, starting transfers between devices, per_device(): lax.all_to_all(outgoing, 'band', split_axis=0, concat_axis=0, tiled=True)  7.81 us
    all_to_all x1, starting transfers between devices, per_device(): lax.all_to_all(serve_blocks(prop_t), 'band', split_axis=0, concat_axis=0,...  7.68 us
    all_to_all x1, starting transfers between devices, per_device(): lax.all_to_all(back_terms, 'band', split_axis=0, concat_axis=0, tiled=True)  7.4 us
  transfers between devices with their start and end apart: 11, of which 2 were waited for; matrix products, arithmetic and copies ran while one was open for 13% of the time, Pallas kernels for 0%

profile of v1, /device:TPU:0, one launch (start us, length us, event | category | flops | bytes accessed | tf_op | source)
XLA Modules:
  0.0 352.8 jit_solution(3209450561910589567)
XLA Ops:
  8.6 8.3 %all-to-all-start = ((s32[16,1,1]{2,1,0:T(1,128)}), s32[16,1,1]{2,1,0:T(1,128)S(1)}, u32[]{:S(2)}, u32[]{:S(2)}) async-start(s32[16,1,1]{2,1,0:T(1,128)} %copy.47), calls=%async_computation | async-start | bytes 16384 | tf_op jit(solution)/shard_map/all_to_all | solution.py:31
  17.7 3.8 %collective-permute-start = (bf16[128,128]{1,0:T(8,128)(2,1)S(1)}, bf16[128,128]{1,0:T(8,128)(2,1)S(1)}, u32[]{:S(2)}, u32[]{:S(2)}) collective-permute-start(bf16[128,128]{1,0:T(8,128)(2,1)S(1)} %get-tuple-element.79), channel_id=1, source_target_pairs={{0,2},{2,4},{4,6},{6,8},{8,10},{10,12},{12,14},{14,16},{16,18},{18... | collective-permute-start | bytes 98312 | tf_op jit(solution)/shard_map/ppermute | solution.py:15
  22.9 2.1 fusion.78
  25.7 4.5 %collective-permute-start.2 = (f32[128,128]{1,0:T(8,128)S(1)}, f32[128,128]{1,0:T(8,128)S(1)}, u32[]{:S(2)}, u32[]{:S(2)}) collective-permute-start(f32[128,128]{1,0:T(8,128)S(1)} %slice_bitcast_fusion.4), channel_id=1, source_target_pairs={{0,2},{2,4},{4,6},{6,8},{8,10},{10,12},{12,14},{14,16},{16,18},{18... | collective-permute-start | bytes 196616 | tf_op jit(solution)/shard_map/ppermute | solution.py:15
  32.8 2.4 fusion.46
  35.3 2.0 copy.55
  38.4 7.4 %all-to-all-start.2 = ((bf16[16,128,128]{2,1,0:T(8,128)(2,1)}), bf16[16,128,128]{2,1,0:T(8,128)(2,1)}, u32[]{:S(2)}, u32[]{:S(2)}) async-start(bf16[16,128,128]{2,1,0:T(8,128)(2,1)} %copy.55), calls=%async_computation.2 | async-start | bytes 1048576 | tf_op jit(solution)/shard_map/all_to_all | solution.py:74
  49.2 2.0 copy.48
  56.2 3.8 %collective-permute-done.3 = f32[128,128]{1,0:T(8,128)S(1)} collective-permute-done((f32[128,128]{1,0:T(8,128)S(1)}, f32[128,128]{1,0:T(8,128)S(1)}, u32[]{:S(2)}, u32[]{:S(2)}) %collective-permute-start.3) | collective-permute-done | bytes 65568 | tf_op jit(solution)/shard_map/ppermute | solution.py:17
  61.5 7.8 %all-to-all-start.1 = ((bf16[16,128,128]{1,2,0:T(8,128)(2,1)}), bf16[16,128,128]{1,2,0:T(8,128)(2,1)}, u32[]{:S(2)}, u32[]{:S(2)}) async-start(bf16[16,128,128]{1,2,0:T(8,128)(2,1)} %broadcast_select_fusion.1), calls=%async_computation.1 | async-start | bytes 1048576 | tf_op jit(solution)/shard_map/all_to_all | solution.py:73
  72.6 3.8 %collective-permute-start.4 = (bf16[128,128]{1,0:T(8,128)(2,1)S(1)}, bf16[128,128]{1,0:T(8,128)(2,1)S(1)}, u32[]{:S(2)}, u32[]{:S(2)}) collective-permute-start(bf16[128,128]{1,0:T(8,128)(2,1)S(1)} %get-tuple-element.75), channel_id=1, source_target_pairs={{0,2},{2,4},{4,6},{6,8},{8,10},{10,12},{12,14},{14,16},{16,18},{18... | collective-permute-start | bytes 98312 | tf_op jit(solution)/shard_map/ppermute | solution.py:15
  77.7 3.2 gather_fusion.4
  82.9 7.7 %all-to-all-start.3 = ((bf16[16,128,128]{2,1,0:T(8,128)(2,1)}), bf16[16,128,128]{2,1,0:T(8,128)(2,1)}, u32[]{:S(2)}, u32[]{:S(2)}) async-start(bf16[16,128,128]{2,1,0:T(8,128)(2,1)} %broadcast_select_fusion), calls=%async_computation.3 | async-start | bytes 1048576 | tf_op jit(solution)/shard_map/all_to_all | solution.py:80
  90.6 2.5 convolution_bitcast_fusion.1
  93.1 2.6 copy.49
  99.7 4.3 %gather_fusion.3 = bf16[1024,128]{1,0:T(8,128)(2,1)} fusion(bf16[2048,128]{1,0:T(8,128)(2,1)S(1)} %bitcast.138, s32[1024]{0:T(1024)S(1)} %fusion.70), kind=kCustom, calls=%fused_computation.1.clone | custom fusion | bytes 528384 | tf_op jit(solution)/shard_map/jit(_take)/gather | solution.py:90
  105.0 2.5 convolution_bitcast_fusion
  107.5 2.6 copy.60
  114.0 3.2 gather_fusion.5
  118.3 4.6 %all_to_all.45 = bf16[3,1024,128]{2,0,1:T(4,128)(2,1)S(1)} all-to-all(bf16[3,1024,128]{2,0,1:T(4,128)(2,1)S(1)} %copy.62), channel_id=1, replica_groups=mesh['band'=16,'dp'=2] {'dp'}, dimensions={1} | all-to-all | bytes 1572864 | tf_op jit(solution)/shard_map/all_to_all | solution.py:96
  125.5 2.5 fusion.3
  130.2 5.0 %fusion.21 = f32[768,1024]{1,0:T(8,128)} fusion(bf16[768,512]{1,0:T(8,128)(2,1)S(1)} %bitcast.145, f32[512,1024,1]{1,0,2:T(8,128)} %get-tuple-element.85, bf16[1024,256]{1,0:T(8,128)(2,1)S(1)} %copy-done.13, f32[512,256]{0,1:T(8,128)S(1)} %get-tuple-element.87, s32[512]{0:T(512)S(1)} %copy-done.21, f32[512]{0:T(512)S(1)} %fusion.56, ...), kind=kOutput, calls=%fused_computation.30 | convolution fusion | flops 1079377920 | bytes 7084032 | tf_op jit(solution)/shard_map/krf,rh->kfh/dot_general | solution.py:115
  135.2 30.0 %all-reduce.6.cloned.1.call-done = (f32[768,1024]{1,0:T(8,128)}, f32[1024,256]{1,0:T(8,128)}) async-done(((f32[768,1024]{1,0:T(8,128)}, f32[1024,256]{1,0:T(8,128)}), (f32[768,1024]{1,0:T(8,128)}, f32[1024,256]{1,0:T(8,128)})) %all-reduce.6.cloned.1.call-update) | async-done | bytes 4194320 | tf_op jit(solution)/shard_map/psum | solution.py:118
  165.2 180.7 %all-reduce.7 = (bf16[768,1024]{1,0:T(8,128)(2,1)}, bf16[1024,256]{1,0:T(8,128)(2,1)}) all-reduce(f32[768,1024]{1,0:T(8,128)} %get-tuple-element.69, f32[1024,256]{1,0:T(8,128)} %get-tuple-element.70), channel_id=1, replica_groups=mesh['band'=16,'dp'=2] {'band'}, use_global_device_ids=true, to_apply=%region_3.6 | all-reduce | flops 1048576 | bytes 6291456 | tf_op jit(solution)/shard_map/psum | solution.py:118
  (101 shorter events, 38.8 us)
Async XLA Ops:
  7.2 118.3 %copy-start = (bf16[768,1024]{1,0:T(8,128)(2,1)S(1)}, bf16[768,1024]{1,0:T(8,128)(2,1)}, u32[]{:S(2)}) copy-start(bf16[768,1024]{1,0:T(8,128)(2,1)} %param.30) | copy-start | bytes 4718596
  8.6 29.7 %all-to-all-start = ((s32[16,1,1]{2,1,0:T(1,128)}), s32[16,1,1]{2,1,0:T(1,128)S(1)}, u32[]{:S(2)}, u32[]{:S(2)}) async-start(s32[16,1,1]{2,1,0:T(1,128)} %copy.47), calls=%async_computation | async-start | bytes 16384 | tf_op jit(solution)/shard_map/all_to_all | solution.py:31
  17.7 37.4 %collective-permute-start = (bf16[128,128]{1,0:T(8,128)(2,1)S(1)}, bf16[128,128]{1,0:T(8,128)(2,1)S(1)}, u32[]{:S(2)}, u32[]{:S(2)}) collective-permute-start(bf16[128,128]{1,0:T(8,128)(2,1)S(1)} %get-tuple-element.79), channel_id=1, source_target_pairs={{0,2},{2,4},{4,6},{6,8},{8,10},{10,12},{12,14},{14,16},{16,18},{18... | collective-permute-start | bytes 98312 | tf_op jit(solution)/shard_map/ppermute | solution.py:15
  21.6 33.6 %collective-permute-start.1 = (bf16[128,128]{1,0:T(8,128)(2,1)S(1)}, bf16[128,128]{1,0:T(8,128)(2,1)S(1)}, u32[]{:S(2)}, u32[]{:S(2)}) collective-permute-start(bf16[128,128]{1,0:T(8,128)(2,1)S(1)} %get-tuple-element.80), channel_id=1, source_target_pairs={{2,0},{4,2},{6,4},{8,6},{10,8},{12,10},{14,12},{16,14},{18,16},{20... | collective-permute-start | bytes 98312 | tf_op jit(solution)/shard_map/ppermute | solution.py:17
  25.5 4.8 %copy-start.18 = (s32[16]{0:T(128)S(1)}, s32[16]{0:T(128)}, u32[]{:S(2)}) copy-start(s32[16]{0:T(128)} %param.26) | copy-start | bytes 196
  25.5 5.3 %copy-start.16 = (s32[1024]{0:T(1024)S(1)}, s32[1024]{0:T(1024)}, u32[]{:S(2)}) copy-start(s32[1024]{0:T(1024)} %param.28) | copy-start | bytes 12292
  25.5 5.9 %copy-start.2 = (bf16[2048,128]{1,0:T(8,128)(2,1)S(1)}, bf16[2048,128]{1,0:T(8,128)(2,1)}, u32[]{:S(2)}) copy-start(bf16[2048,128]{1,0:T(8,128)(2,1)} %param.23) | copy-start | bytes 1572868
  25.7 27.5 %collective-permute-start.2 = (f32[128,128]{1,0:T(8,128)S(1)}, f32[128,128]{1,0:T(8,128)S(1)}, u32[]{:S(2)}, u32[]{:S(2)}) collective-permute-start(f32[128,128]{1,0:T(8,128)S(1)} %slice_bitcast_fusion.4), channel_id=1, source_target_pairs={{0,2},{2,4},{4,6},{6,8},{8,10},{10,12},{12,14},{14,16},{16,18},{18... | collective-permute-start | bytes 196616 | tf_op jit(solution)/shard_map/ppermute | solution.py:15
  38.4 23.1 %all-to-all-start.2 = ((bf16[16,128,128]{2,1,0:T(8,128)(2,1)}), bf16[16,128,128]{2,1,0:T(8,128)(2,1)}, u32[]{:S(2)}, u32[]{:S(2)}) async-start(bf16[16,128,128]{2,1,0:T(8,128)(2,1)} %copy.55), calls=%async_computation.2 | async-start | bytes 1048576 | tf_op jit(solution)/shard_map/all_to_all | solution.py:74
  51.2 18.0 %copy-start.20 = (s32[16]{0:T(128)S(1)}, s32[16]{0:T(128)}, u32[]{:S(2)}) copy-start(s32[16]{0:T(128)} %reduce.10) | copy-start | bytes 196
  53.8 6.1 %collective-permute-start.3 = (f32[128,128]{1,0:T(8,128)S(1)}, f32[128,128]{1,0:T(8,128)S(1)}, u32[]{:S(2)}, u32[]{:S(2)}) collective-permute-start(f32[128,128]{1,0:T(8,128)S(1)} %get-tuple-element.71), channel_id=1, source_target_pairs={{2,0},{4,2},{6,4},{8,6},{10,8},{12,10},{14,12},{16,14},{18,16},{20... | collective-permute-start | bytes 196616 | tf_op jit(solution)/shard_map/ppermute | solution.py:17
  61.5 21.4 %all-to-all-start.1 = ((bf16[16,128,128]{1,2,0:T(8,128)(2,1)}), bf16[16,128,128]{1,2,0:T(8,128)(2,1)}, u32[]{:S(2)}, u32[]{:S(2)}) async-start(bf16[16,128,128]{1,2,0:T(8,128)(2,1)} %broadcast_select_fusion.1), calls=%async_computation.1 | async-start | bytes 1048576 | tf_op jit(solution)/shard_map/all_to_all | solution.py:73
  71.2 40.9 %copy-start.1 = (bf16[16,128,128]{2,1,0:T(8,128)(2,1)}, bf16[16,128,128]{2,1,0:T(8,128)(2,1)S(1)}, u32[]{:S(2)}) copy-start(bf16[16,128,128]{2,1,0:T(8,128)(2,1)S(1)} %fusion.50) | copy-start | bytes 1572868
  72.6 31.3 %collective-permute-start.4 = (bf16[128,128]{1,0:T(8,128)(2,1)S(1)}, bf16[128,128]{1,0:T(8,128)(2,1)S(1)}, u32[]{:S(2)}, u32[]{:S(2)}) collective-permute-start(bf16[128,128]{1,0:T(8,128)(2,1)S(1)} %get-tuple-element.75), channel_id=1, source_target_pairs={{0,2},{2,4},{4,6},{6,8},{8,10},{10,12},{12,14},{14,16},{16,18},{18... | collective-permute-start | bytes 98312 | tf_op jit(solution)/shard_map/ppermute | solution.py:15
  76.4 27.5 %collective-permute-start.5 = (bf16[128,128]{1,0:T(8,128)(2,1)S(1)}, bf16[128,128]{1,0:T(8,128)(2,1)S(1)}, u32[]{:S(2)}, u32[]{:S(2)}) collective-permute-start(bf16[128,128]{1,0:T(8,128)(2,1)S(1)} %get-tuple-element.76), channel_id=1, source_target_pairs={{2,0},{4,2},{6,4},{8,6},{10,8},{12,10},{14,12},{16,14},{18,16},{20... | collective-permute-start | bytes 98312 | tf_op jit(solution)/shard_map/ppermute | solution.py:17
  77.7 12.9 %copy-start.5 = (bf16[16,128,128]{2,1,0:T(8,128)(2,1)S(1)}, bf16[16,128,128]{2,1,0:T(8,128)(2,1)}, u32[]{:S(2)}) copy-start(bf16[16,128,128]{2,1,0:T(8,128)(2,1)} %param.25) | copy-start | bytes 1572868
  82.9 22.1 %all-to-all-start.3 = ((bf16[16,128,128]{2,1,0:T(8,128)(2,1)}), bf16[16,128,128]{2,1,0:T(8,128)(2,1)}, u32[]{:S(2)}, u32[]{:S(2)}) async-start(bf16[16,128,128]{2,1,0:T(8,128)(2,1)} %broadcast_select_fusion), calls=%async_computation.3 | async-start | bytes 1048576 | tf_op jit(solution)/shard_map/all_to_all | solution.py:80
  90.6 5.2 %copy-start.19 = (s32[16]{0:T(128)S(1)}, s32[16]{0:T(128)}, u32[]{:S(2)}) copy-start(s32[16]{0:T(128)} %param.26) | copy-start | bytes 196
  90.6 74.6 %all-reduce.6.cloned.1.call-start = ((), (), s32[]{:S(2)}) async-start(), calls=%async_computation.5 | async-start | bytes 8388608 | tf_op jit(solution)/shard_map/psum | solution.py:118
  99.6 7.9 %copy-start.3 = (bf16[16,128,128]{2,1,0:T(8,128)(2,1)}, bf16[16,128,128]{2,1,0:T(8,128)(2,1)S(1)}, u32[]{:S(2)}) copy-start(bf16[16,128,128]{2,1,0:T(8,128)(2,1)S(1)} %fusion.43) | copy-start | bytes 1572868
  99.6 5.3 %copy-start.6 = (bf16[16,128,128]{2,1,0:T(8,128)(2,1)S(1)}, bf16[16,128,128]{2,1,0:T(8,128)(2,1)}, u32[]{:S(2)}) copy-start(bf16[16,128,128]{2,1,0:T(8,128)(2,1)} %param.25) | copy-start | bytes 1572868
  114.0 3.6 %copy-start.4 = (bf16[16,128,128]{2,1,0:T(8,128)(2,1)}, bf16[16,128,128]{2,1,0:T(8,128)(2,1)S(1)}, u32[]{:S(2)}) copy-start(bf16[16,128,128]{2,1,0:T(8,128)(2,1)S(1)} %fusion.38) | copy-start | bytes 1572868
  114.0 3.2 copy-start.10
  114.0 3.2 copy-start.17
  (9 other events, 16.2 us)
Sparse Core Ops, SparseCore 0:
  135.4 29.8 all-reduce.5
